TPU v7x, 256 devices: a whole 4x4x8 slice. The times are simulated.
256 devices in a mesh: pts: 32 (over x_hi, z, core), dir: 8 (over x_lo, y).
Axes of the slice: x: 4 (x_hi: 2, x_lo: 2; x = x_hi * 2 + x_lo), y: 4, z: 8, core: 2. Of those that a mesh axis runs over, the one named last changes fastest.
Arguments:
- action: float32 [50, 32, 512, 256], P(None, 'dir', 'pts'), may hold values from 0 to 60, as said below
- currents: float32 [2, 512, 256], P(None, 'pts'), may hold values from -0.1 to 0.1, as said below
- land_mask: int32 [512, 256], P('pts'), may hold values 0 or 1
- group_speed: float32 [50], replicated, may hold values from 0.02 to 0.55
- group_ratio: float32 [50], replicated, may hold values from 0.5 to 1
- bin_weight: float32 [50], replicated, may hold values from 0.002 to 0.02
Outputs:
- new_action: float32 [50, 32, 512, 256], P(None, 'dir', 'pts')
- wave_force: float32 [2, 512, 256], P(None, 'pts')
Inputs may be any that keep to these rules, and one draw needn't show every extreme that they name: Positive action densities. currents vary slowly from point to point.
All inputs are finite; a program needn't handle non-finite values. No bound on the sum of `land_mask` on one device may be relied on, other than what follows from the above.
Results may differ from a plain program's by a relative error of at most 0.00022.
Values sent between devices are 32-bit elements; how exact they have to be, the bound alone decides.
No kernel may reach another device: no remote copies, remote signals or barrier semaphores. Data moves between devices by JAX's collectives and lax.ppermute only.
A program may use at most 64 MiB of HBM per device.

v0:
```python
import math
import jax
import jax.numpy as jnp
from jax import lax
from jax.sharding import PartitionSpec as P


def with_halo(value, sides, width, wrap):
    for axis, dim in sides:
        count, length = (lax.axis_size(axis), value.shape[dim])
        up = [(i, (i + 1) % count) for i in range(count if wrap else count - 1)]
        down = [(j, i) for i, j in up]
        last = lax.slice_in_dim(value, length - width, length, axis=dim)
        first = lax.slice_in_dim(value, 0, width, axis=dim)
        before = lax.ppermute(last, axis, up)
        after = lax.ppermute(first, axis, down)
        value = jnp.concatenate([before, value, after], axis=dim)
    return value


def upwind(velocity, behind, in_front):
    return jnp.maximum(velocity, 0.0) * behind + jnp.minimum(velocity, 0.0) * in_front


def advance(extended, cur_u, cur_v, land_cells, cosine_terms, sine_terms, group_speed):
    speed_x = group_speed[:, None, None, None] * cosine_terms[None, :, None, None]
    speed_y = group_speed[:, None, None, None] * sine_terms[None, :, None, None]
    drift_x = speed_x + (0.5 * (cur_u[:-1] + cur_u[1:]))[None, None]
    flux_x = upwind(drift_x, extended[:, :, :-1], extended[:, :, 1:])
    middle = extended[:, :, 1:-1]
    side_v = jnp.pad(cur_v[1:-1], ((0, 0), (1, 1)))
    drift_y = speed_y + (0.5 * (side_v[:, :-1] + side_v[:, 1:]))[None, None]
    padded = jnp.pad(middle, ((0, 0), (0, 0), (0, 0), (1, 1)))
    flux_y = upwind(drift_y, padded[..., :-1], padded[..., 1:])
    change = flux_x[:, :, 1:] - flux_x[:, :, :-1] + (flux_y[..., 1:] - flux_y[..., :-1])
    return land_cells * (middle - change)


def row_slope(values):
    return 0.5 * (values[2:] - values[:-2])


def col_slope(values):
    padded = jnp.pad(values[1:-1], ((0, 0), (1, 1)))
    return 0.5 * (padded[:, 2:] - padded[:, :-2])


def shear_terms(ext_u, ext_v):
    return (row_slope(ext_u), col_slope(ext_u), row_slope(ext_v), col_slope(ext_v))


def turn_rate(face_angles, shears, total_dirs):
    u_dx, u_dy, v_dx, v_dy = shears
    sines = jnp.sin(face_angles)[:, None, None]
    cosines = jnp.cos(face_angles)[:, None, None]
    scale = total_dirs / (2.0 * math.pi)
    return scale * (
        sines * cosines * (u_dx - v_dy) + sines * sines * u_dy - cosines * cosines * v_dx
    )


def refract(cycle_ext, turning):
    flux = upwind(turning[None], cycle_ext[:, :-1], cycle_ext[:, 1:])
    return cycle_ext[:, 1:-1] - (flux[:, 1:] - flux[:, :-1])


def stress_table(angles, bin_weight, group_ratio):
    cos_sq = (jnp.cos(angles) * jnp.cos(angles))[None]
    sin_sq = (jnp.sin(angles) * jnp.sin(angles))[None]
    cross = (jnp.sin(angles) * jnp.cos(angles))[None]
    ratio = group_ratio[:, None]
    weight = bin_weight[:, None]
    return jnp.stack(
        [
            weight * (ratio * (1.0 + cos_sq) - 0.5),
            weight * ratio * cross,
            weight * (ratio * (1.0 + sin_sq) - 0.5),
        ]
    )


def wave_force_of(extended):
    first = -(row_slope(extended[0]) + col_slope(extended[1]))
    second = -(row_slope(extended[1]) + col_slope(extended[2]))
    return jnp.stack([first, second])


def per_device(action, currents, land_mask, group_speed, group_ratio, bin_weight):
    sector_count = action.shape[1]
    total_dirs = sector_count * lax.axis_size("dir")
    step_angle = 2.0 * math.pi / total_dirs
    offset = lax.axis_index("dir") * sector_count
    angles = (offset + jnp.arange(sector_count)).astype(jnp.float32) * step_angle
    cosine_terms = jnp.cos(angles)
    sine_terms = jnp.sin(angles)
    land_cells = land_mask.astype(jnp.float32)
    fields = jnp.stack([currents[0], currents[1], land_cells])
    beside_all = with_halo(fields, (("pts", 1),), 2, False)
    ext_u = beside_all[0, 1:-1]
    ext_v = beside_all[1, 1:-1]
    spectra = land_cells * action
    for substep in range(2):
        extended = with_halo(spectra, (("pts", 2),), 1, False)
        spectra = advance(extended, ext_u, ext_v, land_cells, cosine_terms, sine_terms, group_speed)
    shears = shear_terms(ext_u, ext_v)
    face_angles = ((offset + jnp.arange(sector_count + 1)).astype(jnp.float32) - 0.5) * step_angle
    turning = turn_rate(face_angles, shears, total_dirs)
    cycle_ext = with_halo(spectra, (("dir", 1),), 1, True)
    new_action = refract(cycle_ext, turning)
    partial_value = jnp.einsum(
        "kfd,fdry->kry",
        stress_table(angles, bin_weight, group_ratio),
        new_action,
        precision=lax.Precision.HIGHEST,
    )
    summed = lax.psum(partial_value, "dir")
    extended = with_halo(summed, (("pts", 1),), 1, False)
    return (new_action, wave_force_of(extended))


def solution(mesh):
    in_specs = (P(None, "dir", "pts", None), P(None, "pts", None), P("pts", None), P(), P(), P())
    out_specs = (P(None, "dir", "pts", None), P(None, "pts", None))
    return jax.shard_map(
        per_device, mesh=mesh, in_specs=in_specs, out_specs=out_specs, check_vma=False
    )
```

profile of v0, /device:TPU:6, one launch (start us, length us, event | category | flops | bytes accessed | tf_op | source)
XLA Modules:
  0.0 132.3 jit_solution(10773098734468614222)
XLA Ops:
  0.6 0.7 convert_bitcast_fusion
  1.4 0.7 pad_maximum_fusion.4
  2.1 1.9 %collective-permute-start = (f32[3,2,256]{2,1,0:T(2,128)S(1)}, f32[3,2,256]{2,1,0:T(2,128)S(1)}, u32[]{:S(2)}, u32[]{:S(2)}) collective-permute-start(f32[3,2,256]{2,1,0:T(2,128)S(1)} %get-tuple-element.24), channel_id=1, source_target_pairs={{0,8},{8,16},{16,24},{24,32},{32,40},{40,48},{48,56},{56,64},{64,7... | collective-permute-start | bytes 18440 | tf_op jit(solution)/shard_map/ppermute | solution.py:15
  4.0 8.0 %collective-permute-start.1 = (f32[3,2,256]{2,1,0:T(2,128)S(1)}, f32[3,2,256]{2,1,0:T(2,128)S(1)}, u32[]{:S(2)}, u32[]{:S(2)}) collective-permute-start(f32[3,2,256]{2,1,0:T(2,128)S(1)} %get-tuple-element.25), channel_id=1, source_target_pairs={{8,0},{16,8},{24,16},{32,24},{40,32},{48,40},{56,48},{64,56},{72,6... | collective-permute-start | bytes 18440 | tf_op jit(solution)/shard_map/ppermute | solution.py:16
  12.1 0.0 copy-start.5
  12.1 0.0 copy-start.6
  12.1 0.0 copy-start.7
  12.1 0.0 copy-start.4
  12.1 3.9 %copy_multiply_fusion = f32[50,4,16,256]{3,0,2,1:T(8,128)S(1)} fusion(f32[50,4,16,256]{3,2,1,0:T(8,128)} %param.6, f32[16,256]{1,0:T(8,128)S(1)} %get-tuple-element.30), kind=kLoop, calls=%fused_computation.35 | loop fusion | flops 819200 | bytes 6569984 | tf_op jit(solution)/shard_map/mul | solution.py:101
  16.0 1.8 %copy-done = f32[50,4,16,256]{3,0,2,1:T(8,128)} copy-done((f32[50,4,16,256]{3,0,2,1:T(8,128)}, f32[50,4,16,256]{3,0,2,1:T(8,128)S(1)}, u32[]{:S(2)}) %copy-start) | copy-done | bytes 3276824
  17.8 1.9 %collective-permute-start.2 = (f32[50,4,1,256]{3,0,2,1:T(8,128)S(1)}, f32[50,4,1,256]{3,0,2,1:T(8,128)S(1)}, u32[]{:S(2)}, u32[]{:S(2)}) collective-permute-start(f32[50,4,1,256]{3,0,2,1:T(8,128)S(1)} %get-tuple-element.15), channel_id=1, source_target_pairs={{0,8},{8,16},{16,24},{24,32},{32,40},{40,48},{48,56},{56,64},{64,7... | collective-permute-start | bytes 614408 | tf_op jit(solution)/shard_map/ppermute | solution.py:15
  19.7 7.3 %collective-permute-start.3 = (f32[50,4,1,256]{3,0,2,1:T(8,128)S(1)}, f32[50,4,1,256]{3,0,2,1:T(8,128)S(1)}, u32[]{:S(2)}, u32[]{:S(2)}) collective-permute-start(f32[50,4,1,256]{3,0,2,1:T(8,128)S(1)} %get-tuple-element.14), channel_id=1, source_target_pairs={{8,0},{16,8},{24,16},{32,24},{40,32},{48,40},{56,48},{64,56},{72,6... | collective-permute-start | bytes 614408 | tf_op jit(solution)/shard_map/ppermute | solution.py:16
  27.1 0.1 broadcast_multiply_fusion
  27.2 0.1 broadcast_multiply_fusion.2
  27.4 0.1 fusion.23
  27.4 4.8 %fusion.4 = f32[50,4,16,257]{3,0,2,1:T(8,128)S(1)} fusion(f32[50,4,16,256]{3,0,2,1:T(8,128)} %copy-done, f32[16,257]{1,0:T(8,128)S(1)} %fusion.23, f32[50,4]{0,1:T(4,128)S(1)} %get-tuple-element.34), kind=kLoop, calls=%fused_computation.12 | loop fusion | flops 4934400 | bytes 6583648 | tf_op jit(solution)/shard_map/add | solution.py:22
  32.3 0.0 copy-start.3
  32.3 1.2 fusion.11
  33.5 0.7 copy-done.3
  34.2 5.1 %fusion.19 = f32[50,4,16,256]{3,0,2,1:T(8,128)S(1)} fusion(f32[50,4,16,257]{3,0,2,1:T(8,128)S(1)} %fusion.4, f32[50,4,17,256]{3,0,2,1:T(8,128)S(1)} %fusion.11, f32[16,256]{1,0:T(8,128)S(1)} %get-tuple-element.30, f32[50,4,16,256]{3,2,1,0:T(8,128)S(1)} %copy-done.3), kind=kLoop, calls=%fused_computation.33 | loop fusion | flops 4915200 | bytes 19677184 | tf_op jit(solution)/shard_map/mul | solution.py:36
  39.4 1.9 %collective-permute-start.4 = (f32[50,4,1,256]{3,0,2,1:T(8,128)S(1)}, f32[50,4,1,256]{3,0,2,1:T(8,128)S(1)}, u32[]{:S(2)}, u32[]{:S(2)}) collective-permute-start(f32[50,4,1,256]{3,0,2,1:T(8,128)S(1)} %get-tuple-element.13), channel_id=1, source_target_pairs={{0,8},{8,16},{16,24},{24,32},{32,40},{40,48},{48,56},{56,64},{64,7... | collective-permute-start | bytes 614408 | tf_op jit(solution)/shard_map/ppermute | solution.py:15
  41.3 7.3 %collective-permute-start.5 = (f32[50,4,1,256]{3,0,2,1:T(8,128)S(1)}, f32[50,4,1,256]{3,0,2,1:T(8,128)S(1)}, u32[]{:S(2)}, u32[]{:S(2)}) collective-permute-start(f32[50,4,1,256]{3,0,2,1:T(8,128)S(1)} %get-tuple-element.12), channel_id=1, source_target_pairs={{8,0},{16,8},{24,16},{32,24},{40,32},{48,40},{56,48},{64,56},{72,6... | collective-permute-start | bytes 614408 | tf_op jit(solution)/shard_map/ppermute | solution.py:16
  48.6 3.3 %fusion.5 = f32[50,4,16,257]{3,0,2,1:T(8,128)} fusion(f32[50,4,16,256]{3,0,2,1:T(8,128)S(1)} %fusion.19, f32[16,257]{1,0:T(8,128)S(1)} %fusion.23, f32[50,4]{0,1:T(4,128)S(1)} %get-tuple-element.34), kind=kLoop, calls=%fused_computation.13 | loop fusion | flops 4934400 | bytes 6583648 | tf_op jit(solution)/shard_map/add | solution.py:22
  51.9 0.2 collective-permute-done.5
  52.1 2.5 %fusion.12 = f32[50,4,17,256]{3,0,2,1:T(8,128)} fusion(f32[50,4,16,256]{3,0,2,1:T(8,128)S(1)} %fusion.19, f32[50,4,1,256]{3,0,2,1:T(8,128)S(1)} %collective-permute-done.4, f32[50,4,1,256]{3,0,2,1:T(8,128)S(1)} %collective-permute-done.5, f32[17,256]{1,0:T(8,128)S(1)} %fusion.25, f32[50,4]{0,1:T(4,128)S(1)} %get-tuple-element.33), kind=kLoop, calls=%fused_computation.22 | loop fusion | flops 6963200 | bytes 7186208 | tf_op jit(solution)/shard_map/add | solution.py:22
  54.6 7.5 %fusion.16 = f32[50,4,16,256]{3,0,2,1:T(8,128)S(1)} fusion(f32[50,4,16,256]{3,0,2,1:T(8,128)S(1)} %fusion.19, f32[50,4,16,257]{3,0,2,1:T(8,128)} %fusion.5, f32[50,4,17,256]{3,0,2,1:T(8,128)} %fusion.12, f32[16,256]{1,0:T(8,128)S(1)} %get-tuple-element.30), kind=kLoop, calls=%fused_computation.28 | loop fusion | flops 4096000 | bytes 19677184 | tf_op jit(solution)/shard_map/mul | solution.py:36
  62.1 0.1 fusion.58
  62.2 0.3 copy.35
  62.5 1.7 %collective-permute-start.6 = (f32[50,1,16,256]{3,2,1,0:T(8,128)S(1)}, f32[50,1,16,256]{3,2,1,0:T(8,128)S(1)}, u32[]{:S(2)}, u32[]{:S(2)}) collective-permute-start(f32[50,1,16,256]{3,2,1,0:T(8,128)S(1)} %copy.35), channel_id=1, source_target_pairs={{0,1},{1,2},{2,3},{3,4},{4,5},{5,6},{6,7},{7,0},{8,9},{9,10},{10,1... | collective-permute-start | bytes 2457608 | tf_op jit(solution)/shard_map/ppermute | solution.py:15
  64.1 0.3 copy.37
  64.4 2.8 %collective-permute-start.7 = (f32[50,1,16,256]{3,2,1,0:T(8,128)S(1)}, f32[50,1,16,256]{3,2,1,0:T(8,128)S(1)}, u32[]{:S(2)}, u32[]{:S(2)}) collective-permute-start(f32[50,1,16,256]{3,2,1,0:T(8,128)S(1)} %copy.37), channel_id=1, source_target_pairs={{1,0},{2,1},{3,2},{4,3},{5,4},{6,5},{7,6},{0,7},{9,8},{10,9},{11,1... | collective-permute-start | bytes 2457608 | tf_op jit(solution)/shard_map/ppermute | solution.py:16
  67.3 0.1 add_multiply_fusion.1
  67.4 0.1 fusion.27
  67.5 0.1 fusion.21
  67.6 12.2 %collective-permute-done.6 = f32[50,1,16,256]{3,2,1,0:T(8,128)S(1)} collective-permute-done((f32[50,1,16,256]{3,2,1,0:T(8,128)S(1)}, f32[50,1,16,256]{3,2,1,0:T(8,128)S(1)}, u32[]{:S(2)}, u32[]{:S(2)}) %collective-permute-start.6) | collective-permute-done | bytes 819232 | tf_op jit(solution)/shard_map/ppermute | solution.py:15
  79.8 0.5 copy.36
  80.3 0.5 copy.38
  80.8 1.1 fusion.10
  81.9 0.6 fusion.13
  82.6 1.8 %copy-done.2 = f32[50,4,16,256]{3,0,2,1:T(8,128)} copy-done((f32[50,4,16,256]{3,0,2,1:T(8,128)}, f32[50,4,16,256]{3,0,2,1:T(8,128)S(1)}, u32[]{:S(2)}) %copy-start.2) | copy-done | bytes 3276824
  84.4 1.9 %convolution_bitcast_fusion = f32[3,16,256]{2,0,1:T(4,128)S(1)} fusion(f32[50,4,16,256]{3,0,2,1:T(8,128)S(1)} %fusion.13, f32[3,50,4]{1,2,0:T(4,128)S(1)} %pad_maximum_fusion.5), kind=kOutput, calls=%fused_computation.36 | convolution fusion | flops 29491200 | bytes 3328352 | tf_op jit(solution)/shard_map/kfd,fdry->kry/dot_general | solution.py:110
  86.3 34.8 %psum.7 = f32[3,16,256]{2,0,1:T(4,128)S(1)} all-reduce(f32[3,16,256]{2,0,1:T(4,128)S(1)} %convolution_bitcast_fusion), channel_id=1, replica_groups=mesh['pts'=32,'dir'=8] {'dir'}, use_global_device_ids=true, to_apply=%region_0.1 | all-reduce | flops 12288 | bytes 98304 | tf_op jit(solution)/shard_map/psum | solution.py:116
  121.1 1.9 %collective-permute-start.8 = (f32[3,1,256]{2,1,0:T(1,128)S(1)}, f32[3,1,256]{2,1,0:T(1,128)S(1)}, u32[]{:S(2)}, u32[]{:S(2)}) collective-permute-start(f32[3,1,256]{2,1,0:T(1,128)S(1)} %get-tuple-element.20), channel_id=1, source_target_pairs={{8,0},{16,8},{24,16},{32,24},{40,32},{48,40},{56,48},{64,56},{72,6... | collective-permute-start | bytes 9224 | tf_op jit(solution)/shard_map/ppermute | solution.py:16
  123.1 2.4 %collective-permute-start.9 = (f32[3,1,256]{2,1,0:T(1,128)S(1)}, f32[3,1,256]{2,1,0:T(1,128)S(1)}, u32[]{:S(2)}, u32[]{:S(2)}) collective-permute-start(f32[3,1,256]{2,1,0:T(1,128)S(1)} %get-tuple-element.21), channel_id=1, source_target_pairs={{0,8},{8,16},{16,24},{24,32},{32,40},{40,48},{48,56},{56,64},{64,7... | collective-permute-start | bytes 9224 | tf_op jit(solution)/shard_map/ppermute | solution.py:15
  125.5 4.8 %copy.46 = f32[50,4,16,256]{3,2,1,0:T(8,128)} copy(f32[50,4,16,256]{3,0,2,1:T(8,128)} %copy-done.2) | data formatting | bytes 6553600
  130.4 1.2 collective-permute-done.9
  131.6 0.1 fusion.32
  131.7 0.6 pad_maximum_fusion.1
  (33 shorter events, 0.5 us)
Async XLA Ops:
  2.1 25.2 %collective-permute-start = (f32[3,2,256]{2,1,0:T(2,128)S(1)}, f32[3,2,256]{2,1,0:T(2,128)S(1)}, u32[]{:S(2)}, u32[]{:S(2)}) collective-permute-start(f32[3,2,256]{2,1,0:T(2,128)S(1)} %get-tuple-element.24), channel_id=1, source_target_pairs={{0,8},{8,16},{16,24},{24,32},{32,40},{40,48},{48,56},{56,64},{64,7... | collective-permute-start | bytes 18440 | tf_op jit(solution)/shard_map/ppermute | solution.py:15
  4.0 23.3 %collective-permute-start.1 = (f32[3,2,256]{2,1,0:T(2,128)S(1)}, f32[3,2,256]{2,1,0:T(2,128)S(1)}, u32[]{:S(2)}, u32[]{:S(2)}) collective-permute-start(f32[3,2,256]{2,1,0:T(2,128)S(1)} %get-tuple-element.25), channel_id=1, source_target_pairs={{8,0},{16,8},{24,16},{32,24},{40,32},{48,40},{56,48},{64,56},{72,6... | collective-permute-start | bytes 18440 | tf_op jit(solution)/shard_map/ppermute | solution.py:16
  12.1 15.0 %copy-start.5 = (f32[50]{0:T(128)S(1)}, f32[50]{0:T(128)}, u32[]{:S(2)}) copy-start(f32[50]{0:T(128)} %param.10) | copy-start | bytes 604
  12.1 15.0 %copy-start.6 = (f32[50]{0:T(128)S(1)}, f32[50]{0:T(128)}, u32[]{:S(2)}) copy-start(f32[50]{0:T(128)} %param.11) | copy-start | bytes 604
  12.1 15.1 %copy-start.7 = (f32[50]{0:T(128)S(1)}, f32[50]{0:T(128)}, u32[]{:S(2)}) copy-start(f32[50]{0:T(128)} %param.9) | copy-start | bytes 604
  12.1 15.2 %copy-start.4 = (f32[2,16,256]{2,1,0:T(8,128)S(1)}, f32[2,16,256]{2,1,0:T(8,128)}, u32[]{:S(2)}) copy-start(f32[2,16,256]{2,1,0:T(8,128)} %param.7) | copy-start | bytes 98308
  16.0 1.8 %copy-start = (f32[50,4,16,256]{3,0,2,1:T(8,128)}, f32[50,4,16,256]{3,0,2,1:T(8,128)S(1)}, u32[]{:S(2)}) copy-start(f32[50,4,16,256]{3,0,2,1:T(8,128)S(1)} %copy_multiply_fusion) | copy-start | bytes 9830404
  17.8 14.5 %collective-permute-start.2 = (f32[50,4,1,256]{3,0,2,1:T(8,128)S(1)}, f32[50,4,1,256]{3,0,2,1:T(8,128)S(1)}, u32[]{:S(2)}, u32[]{:S(2)}) collective-permute-start(f32[50,4,1,256]{3,0,2,1:T(8,128)S(1)} %get-tuple-element.15), channel_id=1, source_target_pairs={{0,8},{8,16},{16,24},{24,32},{32,40},{40,48},{48,56},{56,64},{64,7... | collective-permute-start | bytes 614408 | tf_op jit(solution)/shard_map/ppermute | solution.py:15
  19.7 12.6 %collective-permute-start.3 = (f32[50,4,1,256]{3,0,2,1:T(8,128)S(1)}, f32[50,4,1,256]{3,0,2,1:T(8,128)S(1)}, u32[]{:S(2)}, u32[]{:S(2)}) collective-permute-start(f32[50,4,1,256]{3,0,2,1:T(8,128)S(1)} %get-tuple-element.14), channel_id=1, source_target_pairs={{8,0},{16,8},{24,16},{32,24},{40,32},{48,40},{56,48},{64,56},{72,6... | collective-permute-start | bytes 614408 | tf_op jit(solution)/shard_map/ppermute | solution.py:16
  27.4 4.9 %copy-start.1 = (f32[50,4,16,256]{3,0,2,1:T(8,128)S(1)}, f32[50,4,16,256]{3,0,2,1:T(8,128)}, u32[]{:S(2)}) copy-start(f32[50,4,16,256]{3,0,2,1:T(8,128)} %copy-done) | copy-start | bytes 9830404
  32.3 1.9 %copy-start.3 = (f32[50,4,16,256]{3,2,1,0:T(8,128)S(1)}, f32[50,4,16,256]{3,2,1,0:T(8,128)}, u32[]{:S(2)}) copy-start(f32[50,4,16,256]{3,2,1,0:T(8,128)} %param.6) | copy-start | bytes 9830404
  39.4 12.5 %collective-permute-start.4 = (f32[50,4,1,256]{3,0,2,1:T(8,128)S(1)}, f32[50,4,1,256]{3,0,2,1:T(8,128)S(1)}, u32[]{:S(2)}, u32[]{:S(2)}) collective-permute-start(f32[50,4,1,256]{3,0,2,1:T(8,128)S(1)} %get-tuple-element.13), channel_id=1, source_target_pairs={{0,8},{8,16},{16,24},{24,32},{32,40},{40,48},{48,56},{56,64},{64,7... | collective-permute-start | bytes 614408 | tf_op jit(solution)/shard_map/ppermute | solution.py:15
  41.3 10.8 %collective-permute-start.5 = (f32[50,4,1,256]{3,0,2,1:T(8,128)S(1)}, f32[50,4,1,256]{3,0,2,1:T(8,128)S(1)}, u32[]{:S(2)}, u32[]{:S(2)}) collective-permute-start(f32[50,4,1,256]{3,0,2,1:T(8,128)S(1)} %get-tuple-element.12), channel_id=1, source_target_pairs={{8,0},{16,8},{24,16},{32,24},{40,32},{48,40},{56,48},{64,56},{72,6... | collective-permute-start | bytes 614408 | tf_op jit(solution)/shard_map/ppermute | solution.py:16
  62.5 17.3 %collective-permute-start.6 = (f32[50,1,16,256]{3,2,1,0:T(8,128)S(1)}, f32[50,1,16,256]{3,2,1,0:T(8,128)S(1)}, u32[]{:S(2)}, u32[]{:S(2)}) collective-permute-start(f32[50,1,16,256]{3,2,1,0:T(8,128)S(1)} %copy.35), channel_id=1, source_target_pairs={{0,1},{1,2},{2,3},{3,4},{4,5},{5,6},{6,7},{7,0},{8,9},{9,10},{10,1... | collective-permute-start | bytes 2457608 | tf_op jit(solution)/shard_map/ppermute | solution.py:15
  64.4 15.9 %collective-permute-start.7 = (f32[50,1,16,256]{3,2,1,0:T(8,128)S(1)}, f32[50,1,16,256]{3,2,1,0:T(8,128)S(1)}, u32[]{:S(2)}, u32[]{:S(2)}) collective-permute-start(f32[50,1,16,256]{3,2,1,0:T(8,128)S(1)} %copy.37), channel_id=1, source_target_pairs={{1,0},{2,1},{3,2},{4,3},{5,4},{6,5},{7,6},{0,7},{9,8},{10,9},{11,1... | collective-permute-start | bytes 2457608 | tf_op jit(solution)/shard_map/ppermute | solution.py:16
  82.6 1.8 %copy-start.2 = (f32[50,4,16,256]{3,0,2,1:T(8,128)}, f32[50,4,16,256]{3,0,2,1:T(8,128)S(1)}, u32[]{:S(2)}) copy-start(f32[50,4,16,256]{3,0,2,1:T(8,128)S(1)} %fusion.13) | copy-start | bytes 9830404
  121.1 9.2 %collective-permute-start.8 = (f32[3,1,256]{2,1,0:T(1,128)S(1)}, f32[3,1,256]{2,1,0:T(1,128)S(1)}, u32[]{:S(2)}, u32[]{:S(2)}) collective-permute-start(f32[3,1,256]{2,1,0:T(1,128)S(1)} %get-tuple-element.20), channel_id=1, source_target_pairs={{8,0},{16,8},{24,16},{32,24},{40,32},{48,40},{56,48},{64,56},{72,6... | collective-permute-start | bytes 9224 | tf_op jit(solution)/shard_map/ppermute | solution.py:16
  123.1 8.5 %collective-permute-start.9 = (f32[3,1,256]{2,1,0:T(1,128)S(1)}, f32[3,1,256]{2,1,0:T(1,128)S(1)}, u32[]{:S(2)}, u32[]{:S(2)}) collective-permute-start(f32[3,1,256]{2,1,0:T(1,128)S(1)} %get-tuple-element.21), channel_id=1, source_target_pairs={{0,8},{8,16},{16,24},{24,32},{32,40},{40,48},{48,56},{56,64},{64,7... | collective-permute-start | bytes 9224 | tf_op jit(solution)/shard_map/ppermute | solution.py:15
where the time goes:
time: 133 us; the launch traced here: 132 us
  starting transfers between devices  37.1 us (28%)
  blocking collectives  34.8 us (26%)
  other arithmetic  32.9 us (25%)
  waiting for transfers between devices  13.6 us (10%)
  local copies, waits for them, and re-layouts  10.9 us (8%)
  matrix products  1.93 us (1%)
    psum x1, blocking collectives, per_device(): summed = lax.psum(partial_value, 'dir')  34.8 us
    ppermute x5, starting transfers between devices, with_halo(): after = lax.ppermute(first, axis, down)  27.3 us
    ppermute x5, waiting for transfers between devices, with_halo(): before = lax.ppermute(last, axis, up)  13.4 us
    add x5, other arithmetic, upwind(): jnp.maximum(velocity, 0.0) * behind + jnp.minimum(velocity, 0.0) * in_front  13 us
    mul x2, other arithmetic, advance(): return land_cells * (middle - change)  12.6 us
    ppermute x5, starting transfers between devices, with_halo(): before = lax.ppermute(last, axis, up)  9.81 us
    unnamed x19, local copies, waits for them, and re-layouts  9.12 us
    mul x1, other arithmetic, per_device(): spectra = land_cells * action  3.85 us
  transfers between devices with their start and end apart: 10, of which 3 were waited for; matrix products, arithmetic and copies ran while one was open for 14% of the time, Pallas kernels for 0%

commit v1 on v0

--- a/solution.py
+++ b/solution.py
@@ -113,7 +113,7 @@
         new_action,
         precision=lax.Precision.HIGHEST,
     )
-    summed = lax.psum(partial_value, "dir")
+    summed = jnp.sum(lax.all_gather(partial_value, "dir"), axis=0)
     extended = with_halo(summed, (("pts", 1),), 1, False)
     return (new_action, wave_force_of(extended))
 

time: 133 us -> 127 us (0.955)
  blocking collectives: 34.8 us -> 28.6 us
    psum x1 -> x0, blocking collectives: 34.8 us -> none  [per_device(): summed = lax.psum(partial_value, 'dir')]
    all_gather x0 -> x1, blocking collectives: none -> 28.6 us  [per_device(): summed = jnp.sum(lax.all_gather(partial_value, 'dir'), axis=0)]
    unnamed x19 -> x17, local copies, waits for them, and re-layouts: 9.12 us -> 9.11 us
  transfers between devices with their start and end apart: 10 -> 10, of which waited for: 3 -> 3; matrix products, arithmetic and copies ran while one was open for 14% -> 15% of each run, Pallas kernels for 0% -> 0%
where the time goes in v1:
time: 127 us; the launch traced here: 126 us
  starting transfers between devices  37.1 us (29%)
  other arithmetic  33 us (26%)
  blocking collectives  28.6 us (23%)
  waiting for transfers between devices  13.7 us (11%)
  local copies, waits for them, and re-layouts  10.8 us (9%)
  matrix products  1.93 us (2%)
    all_gather x1, blocking collectives, per_device(): summed = jnp.sum(lax.all_gather(partial_value, 'dir'), axis=0)  28.6 us
    ppermute x5, starting transfers between devices, with_halo(): after = lax.ppermute(first, axis, down)  27.3 us
    ppermute x5, waiting for transfers between devices, with_halo(): before = lax.ppermute(last, axis, up)  13.5 us
    add x5, other arithmetic, upwind(): jnp.maximum(velocity, 0.0) * behind + jnp.minimum(velocity, 0.0) * in_front  13 us
    mul x2, other arithmetic, advance(): return land_cells * (middle - change)  12.6 us
    ppermute x5, starting transfers between devices, with_halo(): before = lax.ppermute(last, axis, up)  9.81 us
    unnamed x17, local copies, waits for them, and re-layouts  9.11 us
    mul x1, other arithmetic, per_device(): spectra = land_cells * action  3.85 us
  transfers between devices with their start and end apart: 10, of which 3 were waited for; matrix products, arithmetic and copies ran while one was open for 15% of the time, Pallas kernels for 0%

profile of v1, /device:TPU:6, one launch (start us, length us, event | category | flops | bytes accessed | tf_op | source)
XLA Modules:
  0.0 126.1 jit_solution(16522288837843516729)
XLA Ops:
  0.6 0.7 convert_bitcast_fusion
  1.4 0.7 pad_maximum_fusion.5
  2.1 1.9 %collective-permute-start = (f32[3,2,256]{2,1,0:T(2,128)S(1)}, f32[3,2,256]{2,1,0:T(2,128)S(1)}, u32[]{:S(2)}, u32[]{:S(2)}) collective-permute-start(f32[3,2,256]{2,1,0:T(2,128)S(1)} %get-tuple-element.24), channel_id=1, source_target_pairs={{0,8},{8,16},{16,24},{24,32},{32,40},{40,48},{48,56},{56,64},{64,7... | collective-permute-start | bytes 18440 | tf_op jit(solution)/shard_map/ppermute | solution.py:15
  4.0 8.0 %collective-permute-start.1 = (f32[3,2,256]{2,1,0:T(2,128)S(1)}, f32[3,2,256]{2,1,0:T(2,128)S(1)}, u32[]{:S(2)}, u32[]{:S(2)}) collective-permute-start(f32[3,2,256]{2,1,0:T(2,128)S(1)} %get-tuple-element.25), channel_id=1, source_target_pairs={{8,0},{16,8},{24,16},{32,24},{40,32},{48,40},{56,48},{64,56},{72,6... | collective-permute-start | bytes 18440 | tf_op jit(solution)/shard_map/ppermute | solution.py:16
  12.1 0.0 copy-start.5
  12.1 0.0 copy-start.6
  12.1 0.0 copy-start.7
  12.1 0.0 copy-start.4
  12.1 3.9 %copy_multiply_fusion = f32[50,4,16,256]{3,0,2,1:T(8,128)S(1)} fusion(f32[50,4,16,256]{3,2,1,0:T(8,128)} %param.6, f32[16,256]{1,0:T(8,128)S(1)} %get-tuple-element.30), kind=kLoop, calls=%fused_computation.35 | loop fusion | flops 819200 | bytes 6569984 | tf_op jit(solution)/shard_map/mul | solution.py:101
  16.0 1.8 %copy-done = f32[50,4,16,256]{3,0,2,1:T(8,128)} copy-done((f32[50,4,16,256]{3,0,2,1:T(8,128)}, f32[50,4,16,256]{3,0,2,1:T(8,128)S(1)}, u32[]{:S(2)}) %copy-start) | copy-done | bytes 3276824
  17.8 1.9 %collective-permute-start.2 = (f32[50,4,1,256]{3,0,2,1:T(8,128)S(1)}, f32[50,4,1,256]{3,0,2,1:T(8,128)S(1)}, u32[]{:S(2)}, u32[]{:S(2)}) collective-permute-start(f32[50,4,1,256]{3,0,2,1:T(8,128)S(1)} %get-tuple-element.13), channel_id=1, source_target_pairs={{0,8},{8,16},{16,24},{24,32},{32,40},{40,48},{48,56},{56,64},{64,7... | collective-permute-start | bytes 614408 | tf_op jit(solution)/shard_map/ppermute | solution.py:15
  19.7 7.3 %collective-permute-start.3 = (f32[50,4,1,256]{3,0,2,1:T(8,128)S(1)}, f32[50,4,1,256]{3,0,2,1:T(8,128)S(1)}, u32[]{:S(2)}, u32[]{:S(2)}) collective-permute-start(f32[50,4,1,256]{3,0,2,1:T(8,128)S(1)} %get-tuple-element.12), channel_id=1, source_target_pairs={{8,0},{16,8},{24,16},{32,24},{40,32},{48,40},{56,48},{64,56},{72,6... | collective-permute-start | bytes 614408 | tf_op jit(solution)/shard_map/ppermute | solution.py:16
  27.1 0.1 broadcast_multiply_fusion
  27.2 0.1 broadcast_multiply_fusion.2
  27.4 0.1 fusion.23
  27.4 4.8 %fusion.4 = f32[50,4,16,257]{3,0,2,1:T(8,128)S(1)} fusion(f32[50,4,16,256]{3,0,2,1:T(8,128)} %copy-done, f32[16,257]{1,0:T(8,128)S(1)} %fusion.23, f32[50,4]{0,1:T(4,128)S(1)} %get-tuple-element.34), kind=kLoop, calls=%fused_computation.12 | loop fusion | flops 4934400 | bytes 6583648 | tf_op jit(solution)/shard_map/add | solution.py:22
  32.3 0.0 copy-start.3
  32.3 1.2 fusion.11
  33.5 0.7 copy-done.3
  34.2 5.1 %fusion.19 = f32[50,4,16,256]{3,0,2,1:T(8,128)S(1)} fusion(f32[50,4,16,257]{3,0,2,1:T(8,128)S(1)} %fusion.4, f32[50,4,17,256]{3,0,2,1:T(8,128)S(1)} %fusion.11, f32[16,256]{1,0:T(8,128)S(1)} %get-tuple-element.30, f32[50,4,16,256]{3,2,1,0:T(8,128)S(1)} %copy-done.3), kind=kLoop, calls=%fused_computation.33 | loop fusion | flops 4915200 | bytes 19677184 | tf_op jit(solution)/shard_map/mul | solution.py:36
  39.4 1.9 %collective-permute-start.4 = (f32[50,4,1,256]{3,0,2,1:T(8,128)S(1)}, f32[50,4,1,256]{3,0,2,1:T(8,128)S(1)}, u32[]{:S(2)}, u32[]{:S(2)}) collective-permute-start(f32[50,4,1,256]{3,0,2,1:T(8,128)S(1)} %get-tuple-element.11), channel_id=1, source_target_pairs={{0,8},{8,16},{16,24},{24,32},{32,40},{40,48},{48,56},{56,64},{64,7... | collective-permute-start | bytes 614408 | tf_op jit(solution)/shard_map/ppermute | solution.py:15
  41.3 7.3 %collective-permute-start.5 = (f32[50,4,1,256]{3,0,2,1:T(8,128)S(1)}, f32[50,4,1,256]{3,0,2,1:T(8,128)S(1)}, u32[]{:S(2)}, u32[]{:S(2)}) collective-permute-start(f32[50,4,1,256]{3,0,2,1:T(8,128)S(1)} %get-tuple-element.10), channel_id=1, source_target_pairs={{8,0},{16,8},{24,16},{32,24},{40,32},{48,40},{56,48},{64,56},{72,6... | collective-permute-start | bytes 614408 | tf_op jit(solution)/shard_map/ppermute | solution.py:16
  48.6 3.3 %fusion.5 = f32[50,4,16,257]{3,0,2,1:T(8,128)} fusion(f32[50,4,16,256]{3,0,2,1:T(8,128)S(1)} %fusion.19, f32[16,257]{1,0:T(8,128)S(1)} %fusion.23, f32[50,4]{0,1:T(4,128)S(1)} %get-tuple-element.34), kind=kLoop, calls=%fused_computation.13 | loop fusion | flops 4934400 | bytes 6583648 | tf_op jit(solution)/shard_map/add | solution.py:22
  51.9 0.2 collective-permute-done.5
  52.1 2.5 %fusion.12 = f32[50,4,17,256]{3,0,2,1:T(8,128)} fusion(f32[50,4,16,256]{3,0,2,1:T(8,128)S(1)} %fusion.19, f32[50,4,1,256]{3,0,2,1:T(8,128)S(1)} %collective-permute-done.4, f32[50,4,1,256]{3,0,2,1:T(8,128)S(1)} %collective-permute-done.5, f32[17,256]{1,0:T(8,128)S(1)} %fusion.25, f32[50,4]{0,1:T(4,128)S(1)} %get-tuple-element.33), kind=kLoop, calls=%fused_computation.22 | loop fusion | flops 6963200 | bytes 7186208 | tf_op jit(solution)/shard_map/add | solution.py:22
  54.6 7.5 %fusion.16 = f32[50,4,16,256]{3,0,2,1:T(8,128)S(1)} fusion(f32[50,4,16,256]{3,0,2,1:T(8,128)S(1)} %fusion.19, f32[50,4,16,257]{3,0,2,1:T(8,128)} %fusion.5, f32[50,4,17,256]{3,0,2,1:T(8,128)} %fusion.12, f32[16,256]{1,0:T(8,128)S(1)} %get-tuple-element.30), kind=kLoop, calls=%fused_computation.28 | loop fusion | flops 4096000 | bytes 19677184 | tf_op jit(solution)/shard_map/mul | solution.py:36
  62.1 0.1 fusion.58
  62.2 0.3 copy.24
  62.5 1.7 %collective-permute-start.6 = (f32[50,1,16,256]{3,2,1,0:T(8,128)S(1)}, f32[50,1,16,256]{3,2,1,0:T(8,128)S(1)}, u32[]{:S(2)}, u32[]{:S(2)}) collective-permute-start(f32[50,1,16,256]{3,2,1,0:T(8,128)S(1)} %copy.24), channel_id=1, source_target_pairs={{0,1},{1,2},{2,3},{3,4},{4,5},{5,6},{6,7},{7,0},{8,9},{9,10},{10,1... | collective-permute-start | bytes 2457608 | tf_op jit(solution)/shard_map/ppermute | solution.py:15
  64.1 0.3 copy.26
  64.4 2.8 %collective-permute-start.7 = (f32[50,1,16,256]{3,2,1,0:T(8,128)S(1)}, f32[50,1,16,256]{3,2,1,0:T(8,128)S(1)}, u32[]{:S(2)}, u32[]{:S(2)}) collective-permute-start(f32[50,1,16,256]{3,2,1,0:T(8,128)S(1)} %copy.26), channel_id=1, source_target_pairs={{1,0},{2,1},{3,2},{4,3},{5,4},{6,5},{7,6},{0,7},{9,8},{10,9},{11,1... | collective-permute-start | bytes 2457608 | tf_op jit(solution)/shard_map/ppermute | solution.py:16
  67.3 0.1 add_multiply_fusion.1
  67.4 0.1 fusion.27
  67.5 0.1 fusion.21
  67.6 12.2 %collective-permute-done.6 = f32[50,1,16,256]{3,2,1,0:T(8,128)S(1)} collective-permute-done((f32[50,1,16,256]{3,2,1,0:T(8,128)S(1)}, f32[50,1,16,256]{3,2,1,0:T(8,128)S(1)}, u32[]{:S(2)}, u32[]{:S(2)}) %collective-permute-start.6) | collective-permute-done | bytes 819232 | tf_op jit(solution)/shard_map/ppermute | solution.py:15
  79.8 0.5 copy.25
  80.3 0.5 copy.27
  80.8 1.1 fusion.10
  81.9 0.6 fusion.13
  82.6 1.8 %copy-done.2 = f32[50,4,16,256]{3,0,2,1:T(8,128)} copy-done((f32[50,4,16,256]{3,0,2,1:T(8,128)}, f32[50,4,16,256]{3,0,2,1:T(8,128)S(1)}, u32[]{:S(2)}) %copy-start.2) | copy-done | bytes 3276824
  84.4 1.9 %convolution_bitcast_fusion = f32[3,16,256]{2,0,1:T(4,128)S(1)} fusion(f32[50,4,16,256]{3,0,2,1:T(8,128)S(1)} %fusion.13, f32[3,50,4]{1,2,0:T(4,128)S(1)} %pad_maximum_fusion.6), kind=kOutput, calls=%fused_computation.36 | convolution fusion | flops 29491200 | bytes 3328352 | tf_op jit(solution)/shard_map/kfd,fdry->kry/dot_general | solution.py:110
  86.3 28.6 %all-gather = f32[24,16,256]{2,1,0:T(8,128)S(1)} all-gather(f32[3,16,256]{2,1,0:T(8,128)S(1)} %copy.30), channel_id=2, replica_groups=mesh['pts'=32,'dir'=8] {'dir'}, dimensions={0}, use_global_device_ids=true | all-gather | bytes 442368 | tf_op jit(solution)/shard_map/all_gather | solution.py:116
  115.0 1.9 %collective-permute-start.8 = (f32[3,1,256]{2,1,0:T(1,128)S(1)}, f32[3,1,256]{2,1,0:T(1,128)S(1)}, u32[]{:S(2)}, u32[]{:S(2)}) collective-permute-start(f32[3,1,256]{2,1,0:T(1,128)S(1)} %get-tuple-element.20), channel_id=1, source_target_pairs={{8,0},{16,8},{24,16},{32,24},{40,32},{48,40},{56,48},{64,56},{72,6... | collective-permute-start | bytes 9224 | tf_op jit(solution)/shard_map/ppermute | solution.py:16
  116.9 2.4 %collective-permute-start.9 = (f32[3,1,256]{2,1,0:T(1,128)S(1)}, f32[3,1,256]{2,1,0:T(1,128)S(1)}, u32[]{:S(2)}, u32[]{:S(2)}) collective-permute-start(f32[3,1,256]{2,1,0:T(1,128)S(1)} %get-tuple-element.21), channel_id=1, source_target_pairs={{0,8},{8,16},{16,24},{24,32},{32,40},{40,48},{48,56},{56,64},{64,7... | collective-permute-start | bytes 9224 | tf_op jit(solution)/shard_map/ppermute | solution.py:15
  119.3 4.8 %copy.31 = f32[50,4,16,256]{3,2,1,0:T(8,128)} copy(f32[50,4,16,256]{3,0,2,1:T(8,128)} %copy-done.2) | data formatting | bytes 6553600
  124.1 1.3 %collective-permute-done.9 = f32[3,1,256]{2,1,0:T(1,128)S(1)} collective-permute-done((f32[3,1,256]{2,1,0:T(1,128)S(1)}, f32[3,1,256]{2,1,0:T(1,128)S(1)}, u32[]{:S(2)}, u32[]{:S(2)}) %collective-permute-start.9) | collective-permute-done | bytes 3104 | tf_op jit(solution)/shard_map/ppermute | solution.py:15
  125.4 0.1 fusion.32
  125.5 0.6 pad_maximum_fusion.1
  (31 shorter events, 0.4 us)
Async XLA Ops:
  2.1 25.2 %collective-permute-start = (f32[3,2,256]{2,1,0:T(2,128)S(1)}, f32[3,2,256]{2,1,0:T(2,128)S(1)}, u32[]{:S(2)}, u32[]{:S(2)}) collective-permute-start(f32[3,2,256]{2,1,0:T(2,128)S(1)} %get-tuple-element.24), channel_id=1, source_target_pairs={{0,8},{8,16},{16,24},{24,32},{32,40},{40,48},{48,56},{56,64},{64,7... | collective-permute-start | bytes 18440 | tf_op jit(solution)/shard_map/ppermute | solution.py:15
  4.0 23.3 %collective-permute-start.1 = (f32[3,2,256]{2,1,0:T(2,128)S(1)}, f32[3,2,256]{2,1,0:T(2,128)S(1)}, u32[]{:S(2)}, u32[]{:S(2)}) collective-permute-start(f32[3,2,256]{2,1,0:T(2,128)S(1)} %get-tuple-element.25), channel_id=1, source_target_pairs={{8,0},{16,8},{24,16},{32,24},{40,32},{48,40},{56,48},{64,56},{72,6... | collective-permute-start | bytes 18440 | tf_op jit(solution)/shard_map/ppermute | solution.py:16
  12.1 15.0 %copy-start.5 = (f32[50]{0:T(128)S(1)}, f32[50]{0:T(128)}, u32[]{:S(2)}) copy-start(f32[50]{0:T(128)} %param.10) | copy-start | bytes 604
  12.1 15.0 %copy-start.6 = (f32[50]{0:T(128)S(1)}, f32[50]{0:T(128)}, u32[]{:S(2)}) copy-start(f32[50]{0:T(128)} %param.11) | copy-start | bytes 604
  12.1 15.1 %copy-start.7 = (f32[50]{0:T(128)S(1)}, f32[50]{0:T(128)}, u32[]{:S(2)}) copy-start(f32[50]{0:T(128)} %param.9) | copy-start | bytes 604
  12.1 15.2 %copy-start.4 = (f32[2,16,256]{2,1,0:T(8,128)S(1)}, f32[2,16,256]{2,1,0:T(8,128)}, u32[]{:S(2)}) copy-start(f32[2,16,256]{2,1,0:T(8,128)} %param.7) | copy-start | bytes 98308
  16.0 1.8 %copy-start = (f32[50,4,16,256]{3,0,2,1:T(8,128)}, f32[50,4,16,256]{3,0,2,1:T(8,128)S(1)}, u32[]{:S(2)}) copy-start(f32[50,4,16,256]{3,0,2,1:T(8,128)S(1)} %copy_multiply_fusion) | copy-start | bytes 9830404
  17.8 14.5 %collective-permute-start.2 = (f32[50,4,1,256]{3,0,2,1:T(8,128)S(1)}, f32[50,4,1,256]{3,0,2,1:T(8,128)S(1)}, u32[]{:S(2)}, u32[]{:S(2)}) collective-permute-start(f32[50,4,1,256]{3,0,2,1:T(8,128)S(1)} %get-tuple-element.13), channel_id=1, source_target_pairs={{0,8},{8,16},{16,24},{24,32},{32,40},{40,48},{48,56},{56,64},{64,7... | collective-permute-start | bytes 614408 | tf_op jit(solution)/shard_map/ppermute | solution.py:15
  19.7 12.6 %collective-permute-start.3 = (f32[50,4,1,256]{3,0,2,1:T(8,128)S(1)}, f32[50,4,1,256]{3,0,2,1:T(8,128)S(1)}, u32[]{:S(2)}, u32[]{:S(2)}) collective-permute-start(f32[50,4,1,256]{3,0,2,1:T(8,128)S(1)} %get-tuple-element.12), channel_id=1, source_target_pairs={{8,0},{16,8},{24,16},{32,24},{40,32},{48,40},{56,48},{64,56},{72,6... | collective-permute-start | bytes 614408 | tf_op jit(solution)/shard_map/ppermute | solution.py:16
  27.4 4.9 %copy-start.1 = (f32[50,4,16,256]{3,0,2,1:T(8,128)S(1)}, f32[50,4,16,256]{3,0,2,1:T(8,128)}, u32[]{:S(2)}) copy-start(f32[50,4,16,256]{3,0,2,1:T(8,128)} %copy-done) | copy-start | bytes 9830404
  32.3 1.9 %copy-start.3 = (f32[50,4,16,256]{3,2,1,0:T(8,128)S(1)}, f32[50,4,16,256]{3,2,1,0:T(8,128)}, u32[]{:S(2)}) copy-start(f32[50,4,16,256]{3,2,1,0:T(8,128)} %param.6) | copy-start | bytes 9830404
  39.4 12.5 %collective-permute-start.4 = (f32[50,4,1,256]{3,0,2,1:T(8,128)S(1)}, f32[50,4,1,256]{3,0,2,1:T(8,128)S(1)}, u32[]{:S(2)}, u32[]{:S(2)}) collective-permute-start(f32[50,4,1,256]{3,0,2,1:T(8,128)S(1)} %get-tuple-element.11), channel_id=1, source_target_pairs={{0,8},{8,16},{16,24},{24,32},{32,40},{40,48},{48,56},{56,64},{64,7... | collective-permute-start | bytes 614408 | tf_op jit(solution)/shard_map/ppermute | solution.py:15
  41.3 10.8 %collective-permute-start.5 = (f32[50,4,1,256]{3,0,2,1:T(8,128)S(1)}, f32[50,4,1,256]{3,0,2,1:T(8,128)S(1)}, u32[]{:S(2)}, u32[]{:S(2)}) collective-permute-start(f32[50,4,1,256]{3,0,2,1:T(8,128)S(1)} %get-tuple-element.10), channel_id=1, source_target_pairs={{8,0},{16,8},{24,16},{32,24},{40,32},{48,40},{56,48},{64,56},{72,6... | collective-permute-start | bytes 614408 | tf_op jit(solution)/shard_map/ppermute | solution.py:16
  62.5 17.3 %collective-permute-start.6 = (f32[50,1,16,256]{3,2,1,0:T(8,128)S(1)}, f32[50,1,16,256]{3,2,1,0:T(8,128)S(1)}, u32[]{:S(2)}, u32[]{:S(2)}) collective-permute-start(f32[50,1,16,256]{3,2,1,0:T(8,128)S(1)} %copy.24), channel_id=1, source_target_pairs={{0,1},{1,2},{2,3},{3,4},{4,5},{5,6},{6,7},{7,0},{8,9},{9,10},{10,1... | collective-permute-start | bytes 2457608 | tf_op jit(solution)/shard_map/ppermute | solution.py:15
  64.4 15.9 %collective-permute-start.7 = (f32[50,1,16,256]{3,2,1,0:T(8,128)S(1)}, f32[50,1,16,256]{3,2,1,0:T(8,128)S(1)}, u32[]{:S(2)}, u32[]{:S(2)}) collective-permute-start(f32[50,1,16,256]{3,2,1,0:T(8,128)S(1)} %copy.26), channel_id=1, source_target_pairs={{1,0},{2,1},{3,2},{4,3},{5,4},{6,5},{7,6},{0,7},{9,8},{10,9},{11,1... | collective-permute-start | bytes 2457608 | tf_op jit(solution)/shard_map/ppermute | solution.py:16
  82.6 1.8 %copy-start.2 = (f32[50,4,16,256]{3,0,2,1:T(8,128)}, f32[50,4,16,256]{3,0,2,1:T(8,128)S(1)}, u32[]{:S(2)}) copy-start(f32[50,4,16,256]{3,0,2,1:T(8,128)S(1)} %fusion.13) | copy-start | bytes 9830404
  115.0 9.2 %collective-permute-start.8 = (f32[3,1,256]{2,1,0:T(1,128)S(1)}, f32[3,1,256]{2,1,0:T(1,128)S(1)}, u32[]{:S(2)}, u32[]{:S(2)}) collective-permute-start(f32[3,1,256]{2,1,0:T(1,128)S(1)} %get-tuple-element.20), channel_id=1, source_target_pairs={{8,0},{16,8},{24,16},{32,24},{40,32},{48,40},{56,48},{64,56},{72,6... | collective-permute-start | bytes 9224 | tf_op jit(solution)/shard_map/ppermute | solution.py:16
  116.9 8.5 %collective-permute-start.9 = (f32[3,1,256]{2,1,0:T(1,128)S(1)}, f32[3,1,256]{2,1,0:T(1,128)S(1)}, u32[]{:S(2)}, u32[]{:S(2)}) collective-permute-start(f32[3,1,256]{2,1,0:T(1,128)S(1)} %get-tuple-element.21), channel_id=1, source_target_pairs={{0,8},{8,16},{16,24},{24,32},{32,40},{40,48},{48,56},{56,64},{64,7... | collective-permute-start | bytes 9224 | tf_op jit(solution)/shard_map/ppermute | solution.py:15
